TPU v7x, 256 devices: a whole 4x4x8 slice. The times are simulated.
256 devices in a mesh: seq: 32 (over x, z), head: 8 (over y, core).
Axes of the slice: x: 4, y: 4, z: 8, core: 2. Of those that a mesh axis runs over, the one named last changes fastest.
Arguments:
- queries: bfloat16 [4096, 8192], P('seq', 'head'), may hold values from -250 to 250
- key_vectors: bfloat16 [4096, 1024], P('seq', 'head'), may hold values from -250 to 250
- value_vectors: bfloat16 [4096, 1024], P('seq', 'head'), may hold values from -20 to 20
- positions: int32 [4096], P('seq'), may hold values from 0 to 2047, as said below
- query_map: float32 [64, 128, 128], P('head'), may hold values from -0.5 to 0.5
- key_map: float32 [8, 128, 128], P('head'), may hold values from -0.5 to 0.5
Outputs:
- grad_queries: float32 [4096, 8192], P('seq', 'head')
- grad_keys: float32 [4096, 1024], P('seq', 'head')
- grad_values: float32 [4096, 1024], P('seq', 'head')
- query_map_grad: float32 [64, 128, 128], P('head')
- key_map_grad: float32 [8, 128, 128], P('head')
Inputs may be any that keep to these rules, and one draw needn't show every extreme that they name: positions[0] is 0, and each later position is either 0 (a document begins) or one more than the position before it; the slab holds at most 4 documents, and one of them is exactly 2048 tokens long.
All inputs are finite; a program needn't handle non-finite values.
Results may differ from a plain program's by a relative error of at most 0.0025.
Values may be sent and summed in bfloat16 or wider, within the bound.
No kernel may reach another device: no remote copies, remote signals or barrier semaphores. Data moves between devices by JAX's collectives and lax.ppermute only.
A program may use at most 64 MiB of HBM per device.

v0:
```python
import math
import jax
import jax.numpy as jnp
from jax import lax
from jax.sharding import PartitionSpec as P

HIGHEST = lax.Precision.HIGHEST
NEGATIVE = -1e30
epsilon = 1e-06


def entering(value, axis, join, neutral, backward):
    count, mine = (lax.axis_size(axis), lax.axis_index(axis))
    pieces = jax.tree.map(lambda part: lax.all_gather(part, axis), value)
    if backward:
        pieces = jax.tree.map(lambda part: part[::-1], pieces)
        mine = count - 1 - mine
    running = jax.tree.map(
        lambda part, zero: jnp.full_like(part, 0) + jnp.asarray(zero, part.dtype), value, neutral
    )

    def lap(position, running):
        longer = join(running, jax.tree.map(lambda part: part[position], pieces))
        return jax.tree.map(lambda new, old: jnp.where(position < mine, new, old), longer, running)

    return lax.fori_loop(0, count - 1, lap, running)


def feature_map(logits):
    return jnp.concatenate(
        [jax.nn.softmax(logits, axis=-1), jax.nn.softmax(-logits, axis=-1)], axis=-1
    )


def feature_back(phi, grad_phi, half_width):
    upper = phi[..., :half_width]
    lower = phi[..., half_width:]
    grad_up = grad_phi[..., :half_width]
    grad_low = grad_phi[..., half_width:]
    upper_part = upper * (grad_up - jnp.sum(upper * grad_up, axis=-1, keepdims=True))
    lower_part = lower * (grad_low - jnp.sum(lower * grad_low, axis=-1, keepdims=True))
    return upper_part - lower_part


def chain_states(earlier, later):
    carried = 1.0 - later[2]
    return (
        later[0] + carried * earlier[0],
        later[1] + carried * earlier[1],
        jnp.maximum(earlier[2], later[2]),
    )


def on_device(queries, key_vectors, value_vectors, positions, query_map, key_map):
    tok_rows = queries.shape[0]
    n_group = query_map.shape[0]
    head_dim = key_vectors.shape[1]
    half_width = query_map.shape[2]
    feat_width = 2 * half_width
    my_index = lax.axis_index("seq")
    row_base = my_index * tok_rows
    row_index = row_base + jnp.arange(tok_rows, dtype=jnp.int32)
    starts = row_index - positions
    last_start = starts[-1]
    q_heads = queries.reshape(tok_rows, n_group, head_dim)
    scaling = 1.0 / math.sqrt(head_dim)
    key_float = key_vectors.astype(jnp.float32)
    value_float = value_vectors.astype(jnp.float32)
    key_logits = jnp.dot(key_float, key_map[0], precision=HIGHEST)
    key_phi = feature_map(key_logits)
    initial = (
        jnp.full((n_group, tok_rows), NEGATIVE, jnp.float32),
        jnp.zeros((n_group, tok_rows), jnp.float32),
        jnp.zeros((n_group, tok_rows, head_dim), jnp.float32),
        jnp.zeros((feat_width, head_dim), jnp.float32),
        jnp.zeros((feat_width,), jnp.float32),
    )
    key_block = lax.all_gather(key_vectors, "seq", axis=0, tiled=True)
    value_block = lax.all_gather(value_vectors, "seq", axis=0, tiled=True)
    block_len = key_block.shape[0]
    key_index = jnp.arange(block_len, dtype=jnp.int32)
    visible = (key_index[None, :] <= row_index[:, None]) & (key_index[None, :] >= starts[:, None])

    def update(current):
        run_max, row_sum, summed, state_sum, norm_sums = current
        scores = (
            jnp.einsum("tgd,nd->gtn", q_heads, key_block, preferred_element_type=jnp.float32)
            * scaling
        )
        scores = jnp.where(visible[None], scores, NEGATIVE)
        new_max = jnp.maximum(run_max, jnp.max(scores, axis=-1))
        weights = jnp.where(visible[None], jnp.exp(scores - new_max[..., None]), 0.0)
        row_sum = jnp.sum(weights, axis=-1)
        summed = jnp.einsum(
            "gtn,nd->gtd",
            weights.astype(jnp.bfloat16),
            value_block,
            preferred_element_type=jnp.float32,
        )
        return (new_max, row_sum, summed, state_sum, norm_sums)

    run_max, row_sum, summed, state_sum, norm_sums = lax.cond(
        jnp.any(visible), update, lambda current: current, initial
    )
    held_teacher = jnp.transpose(summed / row_sum[..., None], (1, 0, 2))
    query_float = q_heads.astype(jnp.float32)
    query_logits = jnp.einsum("tgd,gdf->tgf", query_float, query_map, precision=HIGHEST)
    query_phi = feature_map(query_logits)
    visible_rows = (
        (row_index[None, :] <= row_index[:, None]) & (row_index[None, :] >= starts[:, None])
    ).astype(jnp.float32)
    crossing = (starts < row_base).astype(jnp.float32)
    keeping = (starts == last_start).astype(jnp.float32)
    fresh_doc = (last_start >= row_base).astype(jnp.float32).reshape(1)
    kept_phi = key_phi * keeping[:, None]
    state_local = jnp.dot(kept_phi.T, value_float, precision=HIGHEST)
    norms_local = jnp.sum(kept_phi, axis=0)
    state_in, norms_in, unused = entering(
        (state_local, norms_local, fresh_doc),
        "seq",
        chain_states,
        (jnp.zeros_like(state_local), jnp.zeros_like(norms_local), jnp.zeros((1,), jnp.float32)),
        False,
    )
    inner = jnp.einsum("tgf,jf->gtj", query_phi, key_phi, precision=HIGHEST) * visible_rows[None]
    numer = jnp.einsum("gtj,jd->tgd", inner, value_float, precision=HIGHEST)
    numer = numer + crossing[:, None, None] * jnp.einsum(
        "tgf,fd->tgd", query_phi, state_in, precision=HIGHEST
    )
    denom = jnp.sum(inner, axis=-1).T + crossing[:, None] * jnp.einsum(
        "tgf,f->tg", query_phi, norms_in, precision=HIGHEST
    )
    outputs = numer / denom[..., None]
    error = outputs - held_teacher
    grad_numer = error / denom[..., None]
    grad_denom = -jnp.sum(error * outputs, axis=-1) / denom
    mixing = (
        jnp.einsum("tgd,jd->gtj", grad_numer, value_float, precision=HIGHEST)
        + grad_denom.T[:, :, None]
    ) * visible_rows[None]
    grad_qphi = jnp.einsum("gtj,jf->tgf", mixing, key_phi, precision=HIGHEST)
    grad_qphi = grad_qphi + crossing[:, None, None] * (
        jnp.einsum("tgd,fd->tgf", grad_numer, state_in, precision=HIGHEST)
        + grad_denom[..., None] * norms_in
    )
    crossing_phi = query_phi * crossing[:, None, None]
    back_local = jnp.einsum("tgf,tgd->fd", crossing_phi, grad_numer, precision=HIGHEST)
    back_norms = jnp.einsum("tgf,tg->f", crossing_phi, grad_denom, precision=HIGHEST)
    back_in, back_norms_in, unused_flag = entering(
        (back_local, back_norms, fresh_doc),
        "seq",
        chain_states,
        (jnp.zeros_like(back_local), jnp.zeros_like(back_norms), jnp.zeros((1,), jnp.float32)),
        True,
    )
    grad_kphi = jnp.einsum("gtj,tgf->jf", mixing, query_phi, precision=HIGHEST)
    grad_kphi = grad_kphi + keeping[:, None] * (
        jnp.dot(value_float, back_in.T, precision=HIGHEST) + back_norms_in[None, :]
    )
    grad_values = jnp.einsum("gtj,tgd->jd", inner, grad_numer, precision=HIGHEST)
    grad_values = grad_values + keeping[:, None] * jnp.dot(key_phi, back_in, precision=HIGHEST)
    query_dlogit = feature_back(query_phi, grad_qphi, half_width)
    key_dlogit = feature_back(key_phi, grad_kphi, half_width)
    grad_queries = jnp.einsum("tgf,gdf->tgd", query_dlogit, query_map, precision=HIGHEST).reshape(
        tok_rows, n_group * head_dim
    )
    grad_keys = jnp.dot(key_dlogit, key_map[0].T, precision=HIGHEST)
    local_qmap = jnp.einsum("tgd,tgf->gdf", query_float, query_dlogit, precision=HIGHEST)
    local_kmap = jnp.dot(key_float.T, key_dlogit, precision=HIGHEST)[None]
    clip_limit = 0.25 * math.sqrt((n_group + 1) * lax.axis_size("head") * head_dim * half_width)
    summed_qmap, summed_kmap = lax.psum((local_qmap, local_kmap), "seq")
    squared = lax.psum(
        jnp.sum(summed_qmap * summed_qmap) + jnp.sum(summed_kmap * summed_kmap), "head"
    )
    factor = jnp.minimum(1.0, clip_limit / (jnp.sqrt(squared) + epsilon))
    query_map_grad = factor * summed_qmap
    key_map_grad = factor * summed_kmap
    return (grad_queries, grad_keys, grad_values, query_map_grad, key_map_grad)


def solution(mesh):
    placed = (
        P("seq", "head"),
        P("seq", "head"),
        P("seq", "head"),
        P("seq"),
        P("head", None, None),
        P("head", None, None),
    )
    return jax.shard_map(
        on_device,
        mesh=mesh,
        in_specs=placed,
        out_specs=(
            P("seq", "head"),
            P("seq", "head"),
            P("seq", "head"),
            P("head", None, None),
            P("head", None, None),
        ),
        check_vma=False,
    )
```

profile of v0, /device:TPU:1, one launch (start us, length us, event | category | flops | bytes accessed | tf_op | source)
XLA Modules:
  0.0 715.1 jit_solution(13117342215060472636)
XLA Ops:
  14.3 39.5 %all-gather.4 = f32[32,1,256]{2,1,0:T(1,128)S(1)} all-gather(f32[1,1,256]{2,1,0:T(1,128)S(1)} %bitcast.184), channel_id=3, replica_groups=mesh['seq'=32,'head'=8] {'seq'}, dimensions={0}, use_global_device_ids=true | all-gather | bytes 33792 | tf_op jit(solution)/shard_map/all_gather | solution.py:14
  53.8 1.8 copy.60
  59.4 57.9 %all-reduce = f32[32]{0:T(128)S(1)} all-reduce(f32[32]{0:T(128)S(1)} %dynamic-update-slice), channel_id=1, replica_groups=mesh['seq'=32,'head'=8] {'seq'}, use_global_device_ids=true, to_apply=%add | all-reduce | flops 32 | bytes 256
  120.7 2.0 convolution_bitcast_fusion.3
  122.7 39.8 %all-gather.13.cloned.1.call-done = bf16[4096,128]{1,0:T(8,128)(2,1)} async-done(((bf16[128,128]{1,0:T(8,128)(2,1)}), bf16[4096,128]{1,0:T(8,128)(2,1)}) %all-gather.13.cloned.1.call-update) | async-done | bytes 1048592 | tf_op jit(solution)/shard_map/all_gather | solution.py:79
  162.5 12.8 %conditional.1 = (f32[8,128]{1,0:T(8,128)S(1)}, f32[8,128,128]{1,2,0:T(8,128)}) conditional(s32[]{:T(128)} %convert_element_type.26, () %tuple.45, (pred[128,4096]{0,1:T(8,128)(4,1)S(1)}, bf16[4096,128]{1,0:T(8,128)(2,1)}, bf16[128,8,128]{0,2,1:T(8,128)(2,1)}, bf16[4096,128]{1,0:T(8,128)(2,1)}) %tuple.46), branch_computations={%region_13.14_spmd, %region_14.17_spmd} | conditional | flops 2202008576 | bytes 59007020 | solution.py:102
  162.5 3.8 fusion
  166.4 4.8 fusion.3
  171.2 4.0 fusion.2
  175.4 70.9 %all-gather.15.cloned.1.call-done = f32[8192,128]{1,0:T(8,128)} async-done(((f32[256,128]{1,0:T(8,128)}), f32[8192,128]{1,0:T(8,128)}) %all-gather.15.cloned.1.call-update) | async-done | bytes 4194320 | tf_op jit(solution)/shard_map/all_gather | solution.py:14
  246.3 90.0 %while.32 = (s32[]{:T(128)}, f32[256,128]{1,0:T(8,128)S(1)}, f32[256]{0:T(256)S(1)}, s32[]{:T(128)}, f32[32,256,128]{2,1,0:T(8,128)}, /*index=5*/f32[32,1]{0,1:T...) while((s32[]{:T(128)}, f32[256,128]{1,0:T(8,128)S(1)}, f32[256]{0:T(256)S(1)}, s32[]{:T(128)}, ...), condition=%wide.region_10.11_spmd.clone, body=%wide.region_9.10_spmd.clone.sunk | while | flops 132101 | bytes 398487 | solution.py:26
  247.6 1.6 fusion.106
  250.5 1.6 fusion.106
  253.4 1.6 fusion.106
  256.3 1.6 fusion.106
  259.2 1.6 fusion.106
  262.1 1.6 fusion.106
  265.0 1.6 fusion.106
  267.9 1.6 fusion.106
  270.8 1.6 fusion.106
  273.7 1.6 fusion.106
  276.6 1.6 fusion.106
  279.5 1.6 fusion.106
  282.4 1.6 fusion.106
  285.3 1.6 fusion.106
  288.2 1.6 fusion.106
  291.1 1.6 fusion.106
  294.0 1.6 fusion.106
  296.9 1.6 fusion.106
  299.8 1.6 fusion.106
  302.7 1.6 fusion.106
  305.6 1.6 fusion.106
  317.2 1.6 fusion.106
  320.1 1.6 fusion.106
  323.1 1.6 fusion.106
  326.0 1.6 fusion.106
  337.0 2.1 multiply_reduce_fusion.3
  339.0 1.7 convolution_bitcast_fusion.6
  341.8 32.8 %all-gather.5 = f32[32,1,256]{2,1,0:T(1,128)S(1)} all-gather(f32[1,1,256]{2,1,0:T(1,128)S(1)} %convolution_bitcast_fusion.10), channel_id=5, replica_groups=mesh['seq'=32,'head'=8] {'seq'}, dimensions={0}, use_global_device_ids=true | all-gather | bytes 33792 | tf_op jit(solution)/shard_map/all_gather | solution.py:14
  375.7 1.6 convolution_bitcast_fusion.7
  379.7 2.4 convolution_bitcast_fusion.1
  382.1 37.8 %all-gather.17.cloned.1.call-done = f32[8192,128]{1,0:T(8,128)} async-done(((f32[256,128]{1,0:T(8,128)}), f32[8192,128]{1,0:T(8,128)}) %all-gather.17.cloned.1.call-update) | async-done | bytes 4194320 | tf_op jit(solution)/shard_map/all_gather | solution.py:14
  419.9 4.6 rev.9
  424.5 109.9 %while.33 = (s32[]{:T(128)}, f32[256,128]{1,0:T(8,128)S(1)}, f32[256]{0:T(256)S(1)}, s32[]{:T(128)}, f32[32,256,128]{2,1,0:T(8,128)}, /*index=5*/f32[32,1]{0,1:T(1,128)S(1)}, f32[32,256]{1,0:T(8,128)}, s32[]{:T(128)}, s32[]{:T(128)}) while((s32[]{:T(128)}, f32[256,128]{1,0:T(8,128)S(1)}, f32[256]{0:T(256)S(1)}, s32[]{:T(128)}, ...), condition=%wide.region_21.22_spmd.clone, body=%wide.region_20.21_spmd.clone.sunk | while | flops 132101 | bytes 398487 | solution.py:26
  540.4 139.9 %all-reduce.4.cloned.1.call-done = (f32[8,128,128]{1,2,0:T(8,128)}, f32[1,128,128]{1,2,0:T(8,128)}) async-done(((f32[8,128,128]{1,2,0:T(8,128)}, f32[1,128,128]{1,2,0:T(8,128)}), (f32[8,128,128]{1,2,0:T(8,128)}, f32[1,128,128]{1,2,0:T(8,128)})) %all-reduce.4.cloned.1.call-update) | async-done | bytes 589840 | tf_op jit(solution)/shard_map/psum | solution.py:171
  681.7 1.8 multiply_reduce_fusion
  684.8 1.8 fusion.44
  686.6 17.6 %psum.23 = f32[]{:T(128)} all-reduce(f32[]{:T(128)S(6)} %add.151), channel_id=1, replica_groups=mesh['seq'=32,'head'=8] {'head'}, use_global_device_ids=true, to_apply=%region_28.29 | all-reduce | flops 1 | bytes 8 | tf_op jit(solution)/shard_map/psum | solution.py:172
  (291 shorter events, 186.8 us)
Async XLA Ops:
  7.2 110.2 %copy-start = (f32[8,128,128]{2,1,0:T(8,128)S(1)}, f32[8,128,128]{2,1,0:T(8,128)}, u32[]{:S(2)}) copy-start(f32[8,128,128]{2,1,0:T(8,128)} %param.16) | copy-start | bytes 1572868
  7.2 115.5 %all-gather.11.cloned.1.call-start = ((), (), s32[]{:S(2)}) async-start(), calls=%async_computation | async-start | bytes 1081344 | tf_op jit(solution)/shard_map/all_gather | solution.py:78
  7.9 154.6 %all-gather.13.cloned.1.call-start = ((), (), s32[]{:S(2)}) async-start(), calls=%async_computation.1 | async-start | bytes 1081344 | tf_op jit(solution)/shard_map/all_gather | solution.py:79
  8.7 237.7 %all-gather.15.cloned.1.call-start = ((), (), s32[]{:S(2)}) async-start(), calls=%async_computation.2 | async-start | bytes 4325376 | tf_op jit(solution)/shard_map/all_gather | solution.py:14
  13.5 406.4 %all-gather.17.cloned.1.call-start = ((), (), s32[]{:S(2)}) async-start(), calls=%async_computation.3 | async-start | bytes 4325376 | tf_op jit(solution)/shard_map/all_gather | solution.py:14
  162.5 212.7 %copy-start.1 = (bf16[128,128]{1,0:T(8,128)(2,1)S(1)}, bf16[128,128]{1,0:T(8,128)(2,1)}, u32[]{:S(2)}) copy-start(bf16[128,128]{1,0:T(8,128)(2,1)} %param.14) | copy-start | bytes 98308
  162.5 3.8 copy-start.2
  340.7 339.6 %all-reduce.4.cloned.1.call-start = ((), (), s32[]{:S(2)}) async-start(), calls=%async_computation.4 | async-start | bytes 1179648 | tf_op jit(solution)/shard_map/psum | solution.py:171
Sparse Core Ops, SparseCore 0:
  10.6 75.4 all-gather.10
  88.7 73.7 all-gather.12
  165.1 81.1 all-gather.14
  340.8 79.0 all-gather.16
  537.3 142.9 all-reduce.3
where the time goes:
time: 720 us; the launch traced here: 715 us
  waiting for transfers between devices  290 us (40%)
  other arithmetic  190 us (26%)
  blocking collectives  148 us (21%)
  local copies, waits for them, and re-layouts  34.3 us (5%)
  matrix products  34.1 us (5%)
  between operations  17.4 us (2%)
    psum x1, waiting for transfers between devices, on_device(): summed_qmap, summed_kmap = lax.psum((local_qmap, local_kmap), 'seq')  140 us
    select_n x124, other arithmetic, lap(): jnp.where(position < mine, new, old)  140 us
    all_gather x2, waiting for transfers between devices, entering(): pieces = jax.tree.map(lambda part: lax.all_gather(part, axis), value)  109 us
    all_gather x2, blocking collectives, entering(): pieces = jax.tree.map(lambda part: lax.all_gather(part, axis), value)  72.3 us
    unnamed x1, blocking collectives  57.9 us
    all_gather x1, waiting for transfers between devices, on_device(): value_block = lax.all_gather(value_vectors, 'seq', axis=0, tiled=True)  39.8 us
    sub x62, other arithmetic, chain_states(): carried = 1.0 - later[2]  36.6 us
    dynamic_slice x62, local copies, waits for them, and re-layouts, lap(): longer = join(running, jax.tree.map(lambda part: part[position], pieces))  21.9 us
  transfers between devices with their start and end apart: 5, of which 4 were waited for; matrix products, arithmetic and copies ran while one was open for 6% of the time, Pallas kernels for 0%

commit v1 on v0

--- a/solution.py
+++ b/solution.py
@@ -7,6 +7,14 @@
 HIGHEST = lax.Precision.HIGHEST
 NEGATIVE = -1e30
 epsilon = 1e-06
+
+
+def tiled_gather(value, axis, dim):
+    count = lax.axis_size(axis)
+    repeats = [count if d == dim else 1 for d in range(value.ndim)]
+    return lax.all_to_all(
+        jnp.tile(value, repeats), axis, split_axis=dim, concat_axis=dim, tiled=True
+    )
 
 
 def entering(value, axis, join, neutral, backward):
@@ -76,7 +84,7 @@
         jnp.zeros((feat_width,), jnp.float32),
     )
     key_block = lax.all_gather(key_vectors, "seq", axis=0, tiled=True)
-    value_block = lax.all_gather(value_vectors, "seq", axis=0, tiled=True)
+    value_block = tiled_gather(value_vectors, "seq", 0)
     block_len = key_block.shape[0]
     key_index = jnp.arange(block_len, dtype=jnp.int32)
     visible = (key_index[None, :] <= row_index[:, None]) & (key_index[None, :] >= starts[:, None])

time: 720 us -> 649 us (0.901)
  waiting for transfers between devices: 290 us -> 195 us
  starting transfers between devices: 0.2 us -> 12.2 us
  blocking collectives: 148 us -> 156 us
    all_gather x2, waiting for transfers between devices: 109 us -> 55 us  [entering(): pieces = jax.tree.map(lambda part: lax.all_gather(part, axis), value)]
    all_gather x1 -> x0, waiting for transfers between devices: 39.8 us -> none  [on_device(): value_block = lax.all_gather(value_vectors, 'seq', axis=0, tiled=True)]
    all_to_all x0 -> x1, starting transfers between devices: none -> 12 us  [tiled_gather(): lax.all_to_all(jnp.tile(value, repeats), axis, split_axis=dim, concat_axi...]
    all_gather x2, blocking collectives: 72.3 us -> 80.3 us  [entering(): pieces = jax.tree.map(lambda part: lax.all_gather(part, axis), value)]
  transfers between devices with their start and end apart: 5 -> 5, of which waited for: 4 -> 3; matrix products, arithmetic and copies ran while one was open for 6% -> 7% of each run, Pallas kernels for 0% -> 0%
where the time goes in v1:
time: 649 us; the launch traced here: 644 us
  waiting for transfers between devices  195 us (30%)
  other arithmetic  190 us (29%)
  blocking collectives  156 us (24%)
  local copies, waits for them, and re-layouts  36.8 us (6%)
  matrix products  35.2 us (5%)
  between operations  17.4 us (3%)
  starting transfers between devices  12.2 us (2%)
    select_n x124, other arithmetic, lap(): jnp.where(position < mine, new, old)  140 us
    psum x1, waiting for transfers between devices, on_device(): summed_qmap, summed_kmap = lax.psum((local_qmap, local_kmap), 'seq')  140 us
    all_gather x2, blocking collectives, entering(): pieces = jax.tree.map(lambda part: lax.all_gather(part, axis), value)  80.3 us
    unnamed x1, blocking collectives  58.5 us
    all_gather x2, waiting for transfers between devices, entering(): pieces = jax.tree.map(lambda part: lax.all_gather(part, axis), value)  55 us
    sub x62, other arithmetic, chain_states(): carried = 1.0 - later[2]  36.6 us
    dynamic_slice x62, local copies, waits for them, and re-layouts, lap(): longer = join(running, jax.tree.map(lambda part: part[position], pieces))  22.3 us
    psum x1, blocking collectives, on_device(): lax.psum(jnp.sum(summed_qmap * summed_qmap) + jnp.sum(summed_kmap * summe...  17.6 us
  transfers between devices with their start and end apart: 5, of which 3 were waited for; matrix products, arithmetic and copies ran while one was open for 7% of the time, Pallas kernels for 0%

profile of v1, /device:TPU:1, one launch (start us, length us, event | category | flops | bytes accessed | tf_op | source)
XLA Modules:
  0.0 644.3 jit_solution(7642527102291334190)
XLA Ops:
  12.7 2.0 tile.2
  14.7 12.0 %all-to-all-start = ((bf16[32,128,128]{2,1,0:T(8,128)(2,1)}), bf16[32,128,128]{2,1,0:T(8,128)(2,1)}, u32[]{:S(2)}, u32[]{:S(2)}) async-start(bf16[32,128,128]{2,1,0:T(8,128)(2,1)} %tile.2), calls=%async_computation | async-start | bytes 2097152 | tf_op jit(solution)/shard_map/all_to_all | solution.py:15
  27.4 1.8 copy.60
  31.2 48.5 %all-gather.4 = f32[32,1,256]{2,1,0:T(1,128)S(1)} all-gather(f32[1,1,256]{2,1,0:T(1,128)S(1)} %bitcast.185), channel_id=3, replica_groups=mesh['seq'=32,'head'=8] {'seq'}, dimensions={0}, use_global_device_ids=true | all-gather | bytes 33792 | tf_op jit(solution)/shard_map/all_gather | solution.py:22
  81.7 58.5 %all-reduce = f32[32]{0:T(128)S(1)} all-reduce(f32[32]{0:T(128)S(1)} %dynamic-update-slice), channel_id=1, replica_groups=mesh['seq'=32,'head'=8] {'seq'}, use_global_device_ids=true, to_apply=%add | all-reduce | flops 32 | bytes 256
  143.6 2.0 convolution_bitcast_fusion.3
  145.6 13.8 %conditional.1 = (f32[8,128]{1,0:T(8,128)S(1)}, f32[8,128,128]{1,2,0:T(8,128)}) conditional(s32[]{:T(128)} %convert_element_type.26, () %tuple.45, (pred[128,4096]{0,1:T(8,128)(4,1)S(1)}, bf16[4096,128]{1,0:T(8,128)(2,1)}, bf16[128,8,128]{0,2,1:T(8,128)(2,1)}, bf16[32,128,128]{2,1,0:T(8,128)(2,1)}) %tuple.46), branch_computations={%region_13.14_spmd, %region_14.17_spmd} | conditional | flops 2202008576 | bytes 54812688 | solution.py:110
  145.6 3.8 fusion
  149.4 4.0 fusion.2
  153.4 6.0 fusion.3
  159.4 13.3 %all-gather.12.cloned.1.call-done = f32[8192,128]{1,0:T(8,128)} async-done(((f32[256,128]{1,0:T(8,128)}), f32[8192,128]{1,0:T(8,128)}) %all-gather.12.cloned.1.call-update) | async-done | bytes 4194320 | tf_op jit(solution)/shard_map/all_gather | solution.py:22
  172.7 90.2 %while.32 = (s32[]{:T(128)}, f32[256,128]{1,0:T(8,128)S(1)}, f32[256]{0:T(256)S(1)}, s32[]{:T(128)}, f32[32,256,128]{2,1,0:T(8,128)}, /*index=5*/f32[32,1]{0,1:T...) while((s32[]{:T(128)}, f32[256,128]{1,0:T(8,128)S(1)}, f32[256]{0:T(256)S(1)}, s32[]{:T(128)}, ...), condition=%wide.region_10.11_spmd.clone, body=%wide.region_9.10_spmd.clone.sunk | while | flops 132101 | bytes 398487 | solution.py:34
  173.3 1.6 fusion.106
  176.2 1.6 fusion.106
  179.1 1.6 fusion.106
  182.0 1.6 fusion.106
  184.9 1.6 fusion.106
  187.8 1.6 fusion.106
  190.8 1.6 fusion.106
  193.7 1.6 fusion.106
  196.6 1.6 fusion.106
  199.5 1.6 fusion.106
  202.4 1.6 fusion.106
  205.3 1.6 fusion.106
  208.2 1.6 fusion.106
  211.1 1.6 fusion.106
  214.0 1.6 fusion.106
  216.9 1.6 fusion.106
  219.8 1.6 fusion.106
  222.8 1.6 fusion.106
  225.7 1.6 fusion.106
  234.4 1.6 fusion.106
  243.1 1.6 fusion.106
  248.9 1.6 fusion.106
  251.8 1.6 fusion.106
  257.7 1.6 fusion.106
  263.5 2.1 multiply_reduce_fusion.3
  265.6 1.6 convolution_bitcast_fusion.6
  268.4 31.8 %all-gather.5 = f32[32,1,256]{2,1,0:T(1,128)S(1)} all-gather(f32[1,1,256]{2,1,0:T(1,128)S(1)} %convolution_bitcast_fusion.10), channel_id=5, replica_groups=mesh['seq'=32,'head'=8] {'seq'}, dimensions={0}, use_global_device_ids=true | all-gather | bytes 33792 | tf_op jit(solution)/shard_map/all_gather | solution.py:22
  301.2 1.6 convolution_bitcast_fusion.7
  305.2 2.4 convolution_bitcast_fusion.1
  307.6 41.7 %all-gather.14.cloned.1.call-done = f32[8192,128]{1,0:T(8,128)} async-done(((f32[256,128]{1,0:T(8,128)}), f32[8192,128]{1,0:T(8,128)}) %all-gather.14.cloned.1.call-update) | async-done | bytes 4194320 | tf_op jit(solution)/shard_map/all_gather | solution.py:22
  349.3 4.6 rev.9
  353.9 109.8 %while.33 = (s32[]{:T(128)}, f32[256,128]{1,0:T(8,128)S(1)}, f32[256]{0:T(256)S(1)}, s32[]{:T(128)}, f32[32,256,128]{2,1,0:T(8,128)}, /*index=5*/f32[32,1]{0,1:T(1,128)S(1)}, f32[32,256]{1,0:T(8,128)}, s32[]{:T(128)}, s32[]{:T(128)}) while((s32[]{:T(128)}, f32[256,128]{1,0:T(8,128)S(1)}, f32[256]{0:T(256)S(1)}, s32[]{:T(128)}, ...), condition=%wide.region_21.22_spmd.clone, body=%wide.region_20.21_spmd.clone.sunk | while | flops 132101 | bytes 398487 | solution.py:34
  469.7 139.8 %all-reduce.4.cloned.1.call-done = (f32[8,128,128]{1,2,0:T(8,128)}, f32[1,128,128]{1,2,0:T(8,128)}) async-done(((f32[8,128,128]{1,2,0:T(8,128)}, f32[1,128,128]{1,2,0:T(8,128)}), (f32[8,128,128]{1,2,0:T(8,128)}, f32[1,128,128]{1,2,0:T(8,128)})) %all-reduce.4.cloned.1.call-update) | async-done | bytes 589840 | tf_op jit(solution)/shard_map/psum | solution.py:179
  609.5 1.8 multiply_reduce_fusion
  614.0 1.8 fusion.43
  615.8 17.6 %psum.23 = f32[]{:T(128)} all-reduce(f32[]{:T(128)S(6)} %add.151), channel_id=1, replica_groups=mesh['seq'=32,'head'=8] {'head'}, use_global_device_ids=true, to_apply=%region_28.29 | all-reduce | flops 1 | bytes 8 | tf_op jit(solution)/shard_map/psum | solution.py:180
  (289 shorter events, 188.1 us)
Async XLA Ops:
  7.2 133.1 %copy-start = (f32[8,128,128]{2,1,0:T(8,128)S(1)}, f32[8,128,128]{2,1,0:T(8,128)}, u32[]{:S(2)}) copy-start(f32[8,128,128]{2,1,0:T(8,128)} %param.16) | copy-start | bytes 1572868
  7.2 138.4 %all-gather.10.cloned.1.call-start = ((), (), s32[]{:S(2)}) async-start(), calls=%async_computation.1 | async-start | bytes 1081344 | tf_op jit(solution)/shard_map/all_gather | solution.py:86
  7.9 164.8 %all-gather.12.cloned.1.call-start = ((), (), s32[]{:S(2)}) async-start(), calls=%async_computation.2 | async-start | bytes 4325376 | tf_op jit(solution)/shard_map/all_gather | solution.py:22
  14.7 130.9 %all-to-all-start = ((bf16[32,128,128]{2,1,0:T(8,128)(2,1)}), bf16[32,128,128]{2,1,0:T(8,128)(2,1)}, u32[]{:S(2)}, u32[]{:S(2)}) async-start(bf16[32,128,128]{2,1,0:T(8,128)(2,1)} %tile.2), calls=%async_computation | async-start | bytes 2097152 | tf_op jit(solution)/shard_map/all_to_all | solution.py:15
  26.7 322.6 %all-gather.14.cloned.1.call-start = ((), (), s32[]{:S(2)}) async-start(), calls=%async_computation.3 | async-start | bytes 4325376 | tf_op jit(solution)/shard_map/all_gather | solution.py:22
  145.6 155.2 %copy-start.1 = (bf16[128,128]{1,0:T(8,128)(2,1)S(1)}, bf16[128,128]{1,0:T(8,128)(2,1)}, u32[]{:S(2)}) copy-start(bf16[128,128]{1,0:T(8,128)(2,1)} %param.14) | copy-start | bytes 98308
  267.3 342.2 %all-reduce.4.cloned.1.call-start = ((), (), s32[]{:S(2)}) async-start(), calls=%async_computation.4 | async-start | bytes 1179648 | tf_op jit(solution)/shard_map/psum | solution.py:179
Sparse Core Ops, SparseCore 0:
  10.6 78.2 all-gather.9
  91.5 81.1 all-gather.11
  267.4 81.8 all-gather.13
  466.6 142.8 all-reduce.3
